TPU v7x, 256 devices: a whole 4x4x8 slice. The times are simulated.
256 devices in a mesh: layer: 8 (over y, z_lo), dp: 32 (over x, z_hi, core).
Axes of the slice: x: 4, y: 4, z: 8 (z_hi: 4, z_lo: 2; z = z_hi * 2 + z_lo), core: 2. Of those that a mesh axis runs over, the one named last changes fastest.
Arguments:
- states: bfloat16 [24, 64, 32, 32, 128], P('layer', 'dp'), may hold values from -6 to 6
- weights: bfloat16 [24, 1152, 128], P('layer'), may hold values from -0.1875 to 0.1875
- bias: float32 [24, 128], P('layer'), may hold values from -3 to 3
- guesses: float32 [8, 64, 32, 32, 128], P('layer', 'dp'), may hold values from -6 to 6
- coarse_gain: float32 [8, 128], replicated, may hold values from 0.5 to 1
Outputs:
- section_starts: float32 [8, 64, 32, 32, 128], P('layer', 'dp')
- weight_grad: float32 [24, 1152, 128], P('layer', 'dp')
- bias_grad: float32 [24, 128], P('layer', 'dp')
All inputs are finite; a program needn't handle non-finite values.
Results may differ from a plain program's by a relative error of at most 0.007.
Values sent between devices are 32-bit elements; how exact they have to be, the bound alone decides.
No kernel may reach another device: no remote copies, remote signals or barrier semaphores. Data moves between devices by JAX's collectives and lax.ppermute only.
A program may use at most 64 MiB of HBM per device.

v0:
```python
import jax
import jax.numpy as jnp
from jax import lax
from jax.sharding import PartitionSpec as P

step_size = 0.5
layout_names = ("NHWC", "HWIO", "NHWC")


def from_behind(value, axis, steps):
    count = lax.axis_size(axis)
    leading, last = (max(0, -steps), min(count, count - steps))
    return lax.ppermute(value, axis, [(source, source + steps) for source in range(leading, last)])


def prefix_2(shard, axis, combine, identity):
    size, mine = (lax.axis_size(axis), lax.axis_index(axis))
    everything = jax.tree.map(lambda part: lax.all_gather(part, axis), shard)
    start = jax.tree.map(
        lambda part, zero: jnp.broadcast_to(jnp.asarray(zero, part.dtype), part.shape),
        shard,
        identity,
    )

    def hop(k, before):
        at = size - 1 - k
        reached = at > mine
        new = combine(before, jax.tree.map(lambda part: part[at], everything))
        return jax.tree.map(lambda a, b: jnp.where(reached, a, b), new, before)

    return lax.fori_loop(0, size, hop, start)


def as_kernel(matrix):
    channels = matrix.shape[1]
    return matrix.reshape(3, 3, channels, channels)


def convolve(field, kernel):
    return lax.conv_general_dilated(
        field,
        kernel,
        (1, 1),
        ((1, 1), (1, 1)),
        dimension_numbers=layout_names,
        preferred_element_type=jnp.float32,
    )


def transpose_conv(scaled, matrix):
    kernel = jnp.swapaxes(as_kernel(matrix)[::-1, ::-1], 2, 3)
    return convolve(scaled, kernel)


def weight_term(field, scaled):
    height = field.shape[1]
    breadth = field.shape[2]
    padded = jnp.pad(field, ((0, 0), (1, 1), (1, 1), (0, 0)))
    blocks = []
    for row_tap in range(3):
        for col_tap in range(3):
            window = padded[:, row_tap : row_tap + height, col_tap : col_tap + breadth, :]
            blocks.append(
                lax.dot_general(
                    window,
                    scaled,
                    (((0, 1, 2), (0, 1, 2)), ((), ())),
                    preferred_element_type=jnp.float32,
                )
            )
    return jnp.concatenate(blocks, axis=0)


def slopes(field, matrix, offset):
    value = jnp.tanh(convolve(field, as_kernel(matrix)) + offset)
    return 1.0 - value * value


def relax(adjoint, derivs, weights):
    for position in reversed(range(len(derivs))):
        scaled = (derivs[position] * adjoint).astype(jnp.bfloat16)
        adjoint = adjoint + step_size * transpose_conv(scaled, weights[position])
    return adjoint


def per_device(states, weights, bias, guesses, coarse_gain):
    section = lax.axis_index("layer")
    depth = states.shape[0]
    scale = step_size / (states.shape[1] * lax.axis_size("dp"))
    derivs = [
        slopes(states[position], weights[position], bias[position]) for position in range(depth)
    ]
    start_guess = guesses[0]
    first = relax(start_guess, derivs, weights)
    earlier_guess = from_behind(start_guess, "layer", 1)
    residual = jnp.where(section == 0, jnp.zeros_like(first), first - earlier_guess)
    gain_index = jnp.maximum(section - 1, 0)
    own_gain = lax.dynamic_slice_in_dim(coarse_gain, gain_index, 1, 0)[0]

    def compose(earlier, later):
        return (later[0] * earlier[0], later[1] + later[0] * earlier[1])

    identity = (jnp.ones_like(own_gain), jnp.zeros_like(residual))
    prefix = prefix_2((own_gain, residual), "layer", compose, identity)
    correction = prefix[1]
    adjoint = start_guess + correction
    weight_rows = [None] * depth
    bias_rows = [None] * depth
    for position in reversed(range(depth)):
        scaled = (derivs[position] * adjoint).astype(jnp.bfloat16)
        adjoint = adjoint + step_size * transpose_conv(scaled, weights[position])
        weight_part = scale * weight_term(states[position], scaled)
        bias_part = scale * jnp.sum(scaled, axis=(0, 1, 2), dtype=jnp.float32)
        weight_rows[position] = weight_part
        bias_rows[position] = bias_part
    weight_grad = jnp.stack(weight_rows)
    bias_grad = jnp.stack(bias_rows)
    weight_grad, bias_grad = (
        lax.psum_scatter(weight_grad, "dp", scatter_dimension=1, tiled=True),
        lax.psum_scatter(bias_grad, "dp", scatter_dimension=1, tiled=True),
    )
    return (adjoint[None], weight_grad, bias_grad)


def solution(mesh):
    return jax.shard_map(
        per_device,
        mesh=mesh,
        in_specs=(
            P("layer", "dp", None, None, None),
            P("layer", None, None),
            P("layer", None),
            P("layer", "dp", None, None, None),
            P(),
        ),
        out_specs=(P("layer", "dp", None, None, None), P("layer", "dp", None), P("layer", "dp")),
        check_vma=False,
    )
```

profile of v0, /device:TPU:8, one launch (start us, length us, event | category | flops | bytes accessed | tf_op | source)
XLA Modules:
  0.0 558.8 jit_solution(3841809794160389465)
XLA Ops:
  7.2 2.9 copy.275
  10.2 3.8 collective-permute-start
  14.0 1.5 slice_bitcast_fusion.10
  17.7 1.7 fusion.27
  21.5 1.7 fusion.15
  24.0 1.7 fusion.26
  27.5 1.7 fusion.14
  30.2 1.8 fusion.25
  33.6 1.7 fusion.13
  35.4 1.5 copy.93
  38.2 2.9 fusion.61
  41.0 1.6 copy.94
  42.7 16.3 %all-gather.1 = f32[8,1,128]{2,1,0:T(1,128)S(1)} all-gather(f32[1,1,128]{2,1,0:T(1,128)S(1)} %dynamic-slice_bitcast_fusion.1), channel_id=1, replica_groups=mesh['layer'=8,'dp'=32] {'layer'}, dimensions={0}, use_global_device_ids=true | all-gather | bytes 4608 | tf_op jit(solution)/shard_map/all_gather | solution.py:18
  59.1 157.5 %all-gather.4.cloned.1.call-done = f32[16,32,32,128]{3,2,1,0:T(8,128)} async-done(((f32[2,32,32,128]{3,2,1,0:T(8,128)}), f32[16,32,32,128]{3,2,1,0:T(8,128)}) %all-gather.4.cloned.1.call-update) | async-done | bytes 8388624 | tf_op jit(solution)/shard_map/all_gather | solution.py:18
  216.6 15.1 %while.16 = (s32[]{:T(128)}, f32[2,32,32,128]{3,2,1,0:T(8,128)S(1)}, s32[]{:T(128)}, f32[8,2,32,32,128]{4,3,2,1,0:T(8,128)}, f32[8,128]{1,0:T(8,128)S(1)}, /*index=5*/s32[]{:T(128)}, s32[]{:T(128)}, s32[]{:T(128)}, s32[]{:T(128)}) while((s32[]{:T(128)}, f32[2,32,32,128]{3,2,1,0:T(8,128)S(1)}, s32[]{:T(128)}, ...), condition=%wide.region_1.2_spmd.clone, body=%wide.region_0.1_spmd.clone.sunk | while | flops 1048584 | bytes 3147431 | solution.py:31
  216.6 1.8 fusion.160
  218.5 1.8 fusion.160
  220.3 1.8 fusion.160
  222.2 1.8 fusion.160
  224.1 1.8 fusion.160
  225.9 1.8 fusion.160
  227.8 1.8 fusion.160
  229.7 1.8 fusion.160
  231.7 2.5 convert_reduce_fusion
  235.2 1.7 fusion.12
  238.3 1.4 convert_reduce_fusion.1
  240.7 1.7 fusion.11
  263.5 1.7 fusion.10
  266.0 1.6 copy.129
  267.6 74.6 %all-reduce.4 = f32[3,128]{1,0:T(4,128)S(1)} all-reduce(f32[3,128]{1,0:T(4,128)S(1)} %pad_maximum_fusion.1), channel_id=4, replica_groups=mesh['layer'=8,'dp'=32] {'dp'}, use_global_device_ids=true, to_apply=%region_6.7.clone | all-reduce | flops 384 | bytes 3072
  342.9 207.1 %all-reduce.7.cloned.1.call-done = f32[3,1152,128]{2,1,0:T(8,128)} async-done(((f32[3,1152,128]{2,1,0:T(8,128)}), f32[3,1152,128]{2,1,0:T(8,128)}) %all-reduce.7.cloned.1.call-update) | async-done | bytes 1769488
  550.0 1.5 constant_dynamic-slice_fusion.1
  (143 shorter events, 34.8 us)
Async XLA Ops:
  7.2 35.5 %copy-start = (f32[8,128]{1,0:T(8,128)S(1)}, f32[8,128]{1,0:T(8,128)}, u32[]{:S(2)}) copy-start(f32[8,128]{1,0:T(8,128)} %param.11) | copy-start | bytes 12292
  7.2 6.8 %copy-start.10 = (bf16[3,2,32,32,128]{4,3,2,1,0:T(8,128)(2,1)S(1)}, bf16[3,2,32,32,128]{4,3,2,1,0:T(8,128)(2,1)}, u32[]{:S(2)}) copy-start(bf16[3,2,32,32,128]{4,3,2,1,0:T(8,128)(2,1)} %param.7) | copy-start | bytes 4718596
  7.2 209.4 %all-gather.4.cloned.1.call-start = ((), (), s32[]{:S(2)}) async-start(), calls=%async_computation | async-start | bytes 9437184 | tf_op jit(solution)/shard_map/all_gather | solution.py:18
  10.2 28.0 %collective-permute-start = (f32[2,32,32,128]{3,1,2,0:T(8,128)}, f32[2,32,32,128]{3,1,2,0:T(8,128)}, u32[]{:S(2)}, u32[]{:S(2)}) collective-permute-start(f32[2,32,32,128]{3,1,2,0:T(8,128)} %bitcast.426), channel_id=1, source_target_pairs={{0,32},{32,64},{64,96},{96,128},{128,160},{160,192},{192,224},{1,3... | collective-permute-start | bytes 3145736 | tf_op jit(solution)/shard_map/ppermute | solution.py:13
  15.8 1.2 copy-start.11
  17.0 0.7 copy-start.21
  17.0 0.7 copy-start.23
  17.7 3.8 copy-start.19
  17.7 9.8 %copy-start.17 = (bf16[1,1152,128]{2,1,0:T(8,128)(2,1)}, bf16[1,1152,128]{2,1,0:T(8,128)(2,1)S(1)}, u32[]{:S(2)}) copy-start(bf16[1,1152,128]{2,1,0:T(8,128)(2,1)S(1)} %get-tuple-element.190) | copy-start | bytes 884740
  17.7 16.0 %copy-start.15 = (bf16[1,1152,128]{2,1,0:T(8,128)(2,1)}, bf16[1,1152,128]{2,1,0:T(8,128)(2,1)S(1)}, u32[]{:S(2)}) copy-start(bf16[1,1152,128]{2,1,0:T(8,128)(2,1)S(1)} %get-tuple-element.189) | copy-start | bytes 884740
  19.4 1.2 copy-start.2
  19.9 1.4 copy-start.6
  26.2 1.1 copy-start.3
  29.7 2.8 copy-start.5
  32.4 1.1 copy-start.7
  42.6 507.4 %all-reduce.7.cloned.1.call-start = ((), (), s32[]{:S(2)}) async-start(), calls=%async_computation.1 | async-start | bytes 3538944
  234.3 1.0 copy-start.20
  237.0 1.3 copy-start.4
  239.7 1.0 copy-start.18
  242.4 1.3 copy-start.8
  243.7 1.0 copy-start.14
  244.2 3.7 copy-start.9
  248.0 1.0 copy-start.13
  252.6 1.0 copy-start.12
  258.8 0.7 copy-start.22
  262.5 1.0 copy-start.16
  265.6 285.9 %copy-start.1 = (f32[8,128]{1,0:T(8,128)S(1)}, f32[8,128]{1,0:T(8,128)}, u32[]{:S(2)}) copy-start(f32[8,128]{1,0:T(8,128)} %param.11) | copy-start | bytes 12292
Sparse Core Ops, SparseCore 0:
  42.8 173.7 all-gather.3
  259.0 290.9 all-reduce.6
where the time goes:
time: 569 us; the launch traced here: 559 us
  waiting for transfers between devices  366 us (64%)
  blocking collectives  90.9 us (16%)
  local copies, waits for them, and re-layouts  27.4 us (5%)
  matrix products  26.9 us (5%)
  other arithmetic  26.6 us (5%)
  between operations  16.5 us (3%)
    unnamed x3, waiting for transfers between devices  207 us
    all_gather x1, waiting for transfers between devices, prefix_2(): everything = jax.tree.map(lambda part: lax.all_gather(part, axis), shard)  158 us
    unnamed x1, blocking collectives  74.6 us
    unnamed x57, local copies, waits for them, and re-layouts  17.6 us
    all_gather x1, blocking collectives, prefix_2(): everything = jax.tree.map(lambda part: lax.all_gather(part, axis), shard)  16.3 us
    conv_general_dilated x9, matrix products, convolve(): lax.conv_general_dilated(field, kernel, (1, 1), ((1, 1), (1, 1)), dimensi...  15.7 us
    select_n x8, other arithmetic, hop(): return jax.tree.map(lambda a, b: jnp.where(reached, a, b), new, before)  14.5 us
  transfers between devices with their start and end apart: 3, of which 3 were waited for; matrix products, arithmetic and copies ran while one was open for 5% of the time, Pallas kernels for 0%

commit v1 on v0

v1 whole, which is shorter than its diff:
```python
import functools

import jax
import jax.numpy as jnp
from jax import lax
from jax.experimental import pallas as pl
from jax.experimental.pallas import tpu as pltpu
from jax.sharding import PartitionSpec as P

CH = 128
SIDE = 32
PAIRS = SIDE // 2
DEPTH = 3
TAPS = 9 * CH
TRIPLE = 3 * CH
STEP = 0.5
BLOCK = 8
CHUNKS = PAIRS // BLOCK
ROWS = 36
SLAB = 40
f32 = jnp.float32
bf16 = jnp.bfloat16


def dot(a, b):
    return jnp.dot(a, b, preferred_element_type=f32)


def for_chunks(images, body):
    def one(at, carry):
        body(at // CHUNKS, (at % CHUNKS) * BLOCK)
        return carry

    lax.fori_loop(0, images * CHUNKS, one, 0)


def clear_edges(ref):
    images = ref.shape[0]
    zero = jnp.zeros((images, 1, SIDE, TRIPLE), bf16)
    ref[:, 0:1, :, 0:TRIPLE] = zero
    ref[:, PAIRS : PAIRS + 1, :, TRIPLE:] = zero


def spread(ref, image, pair, half, value):
    rows = value.shape[0]
    column = lax.broadcasted_iota(jnp.int32, value.shape, 0) & (SIDE - 1)
    left = jnp.where(column == 0, 0.0, pltpu.roll(value, 1, 0))
    right = jnp.where(column == SIDE - 1, 0.0, pltpu.roll(value, rows - 1, 0))
    base = (1 - half) * TRIPLE
    for at, part in enumerate((left, value, right)):
        lanes = slice(base + at * CH, base + (at + 1) * CH)
        ref[image, pl.ds(pair + half, rows // SIDE), :, lanes] = part.astype(bf16).reshape(-1, SIDE, CH)


def convolve(ref, image, pair, kernel):
    upper = ref[image, pl.ds(pair, BLOCK)].reshape(BLOCK * SIDE, 2 * TRIPLE)
    lower = ref[image, pl.ds(pair + 1, BLOCK)].reshape(BLOCK * SIDE, 2 * TRIPLE)
    return dot(upper, kernel[0 : 2 * TRIPLE, :]) + dot(lower, kernel[2 * TRIPLE :, :])


def fill_kernels(weights, layer, forward, adjoint):
    zero = jnp.zeros((TRIPLE, CH), bf16)
    for row in range(4):
        for half in range(2):
            lanes = slice(half * CH, (half + 1) * CH)
            tap = row - half
            if not 0 <= tap <= 2:
                if forward is not None:
                    forward[row * TRIPLE : (row + 1) * TRIPLE, lanes] = zero
                adjoint[layer, row * TRIPLE : (row + 1) * TRIPLE, lanes] = zero
            elif forward is not None:
                forward[row * TRIPLE : (row + 1) * TRIPLE, lanes] = weights[
                    layer, tap * TRIPLE : (tap + 1) * TRIPLE, :
                ]
    for tap in range(3):
        for side in range(3):
            source = ((2 - tap) * 3 + 2 - side) * CH
            turned = weights[layer, source : source + CH, :].T
            for half in range(2):
                row = (tap + half) * TRIPLE + side * CH
                adjoint[layer, row : row + CH, half * CH : (half + 1) * CH] = turned


def first_kernel(
    states, weights, bias, guess, gain, sent, slope, adjoint_kernels, field, patches, forward, adjoint
):
    images = guess.shape[0]
    clear_edges(field)
    clear_edges(patches)
    for layer in reversed(range(DEPTH)):
        fill_kernels(weights, layer, forward, adjoint_kernels)
        offset = bias[layer : layer + 1, :]

        def gather(image, pair):
            for half in range(2):
                value = states[layer, image, pl.ds(pair, BLOCK), half].reshape(BLOCK * SIDE, CH)
                spread(field, image, pair, half, value.astype(f32))

        for_chunks(images, gather)

        def derive(image, pair):
            both = convolve(field, image, pair, forward)
            for half in range(2):
                lanes = slice(half * CH, (half + 1) * CH)
                value = jnp.tanh(both[:, lanes] + offset)
                value = 1.0 - value * value
                slope[layer, image, pl.ds(pair, BLOCK), :, lanes] = value.reshape(BLOCK, SIDE, CH)
                if layer == DEPTH - 1:
                    now = guess[image, pl.ds(pair, BLOCK), half]
                else:
                    now = adjoint[image, pl.ds(pair, BLOCK), :, lanes]
                spread(patches, image, pair, half, value * now.reshape(BLOCK * SIDE, CH))

        for_chunks(images, derive)

        def back(image, pair):
            both = convolve(patches, image, pair, adjoint_kernels.at[layer])
            for half in range(2):
                lanes = slice(half * CH, (half + 1) * CH)
                change = STEP * both[:, lanes].reshape(BLOCK, SIDE, CH)
                if layer == DEPTH - 1:
                    now = guess[image, pl.ds(pair, BLOCK), half]
                else:
                    now = adjoint[image, pl.ds(pair, BLOCK), :, lanes]
                if layer:
                    adjoint[image, pl.ds(pair, BLOCK), :, lanes] = now + change
                else:
                    old = guess[image, pl.ds(pair, BLOCK), half]
                    sent[image, pl.ds(pair, BLOCK), half] = now + change - gain[...].reshape(1, 1, CH) * old

        for_chunks(images, back)


def second_kernel(
    flags, states, guess, begun, slope, adjoint_kernels, start, mine, other, patches, adjoint, grads, sums, scale
):
    images = guess.shape[0]
    clear_edges(patches)
    last = flags[0] != 0
    core = flags[1]
    for layer in reversed(range(DEPTH)):
        sums[...] = jnp.zeros_like(sums)

        def derive(image, pair):
            for half in range(2):
                lanes = slice(half * CH, (half + 1) * CH)
                if layer == DEPTH - 1:
                    now = jnp.where(
                        last, guess[image, pl.ds(pair, BLOCK), half], begun[image, pl.ds(pair, BLOCK), half]
                    )
                    adjoint[image, pl.ds(pair, BLOCK), :, lanes] = now
                else:
                    now = adjoint[image, pl.ds(pair, BLOCK), :, lanes]
                value = slope[layer, image, pl.ds(pair, BLOCK), :, lanes] * now
                value = value.reshape(BLOCK * SIDE, CH).astype(bf16).astype(f32)
                sums[...] += value.reshape(-1, 8, CH).sum(axis=0)
                spread(patches, image, pair, half, value)

        for_chunks(images, derive)

        def back(image, pair):
            both = convolve(patches, image, pair, adjoint_kernels.at[layer])
            for half in range(2):
                lanes = slice(half * CH, (half + 1) * CH)
                change = STEP * both[:, lanes].reshape(BLOCK, SIDE, CH)
                now = adjoint[image, pl.ds(pair, BLOCK), :, lanes]
                if layer:
                    adjoint[image, pl.ds(pair, BLOCK), :, lanes] = now + change
                else:
                    start[image, pl.ds(pair, BLOCK), half] = now + change

        for_chunks(images, back)

        points = images * PAIRS * SIDE
        halves = [states[layer, :, :, half].reshape(points, CH) for half in range(2)]
        field = jnp.concatenate(halves, axis=1)
        for group in range(2):
            for third in range(3):
                lanes = slice(third * 2 * CH, (third + 1) * 2 * CH)
                part = patches[:, group : group + PAIRS, :, lanes].reshape(points, 2 * CH)
                result = lax.dot_general(field, part, (((0,), (0,)), ((), ())), preferred_element_type=f32)
                for piece in range(2):
                    at = third * 2 + piece
                    row, side = divmod(at, 3)
                    for half in range(2):
                        tap = row + 2 * group - half
                        if not 0 <= tap <= 2:
                            continue
                        block = ((2 - tap) * 3 + 2 - side) * CH
                        value = result[half * CH : (half + 1) * CH, piece * CH : (piece + 1) * CH] * scale
                        fresh = (group, row, half) in ((0, 0, 0), (0, 1, 0), (1, 0, 0))
                        if fresh:
                            grads[block : block + CH, :] = value
                        else:
                            grads[block : block + CH, :] += value
        total = scale * jnp.sum(sums[...], axis=0, keepdims=True)
        tail = jnp.broadcast_to(total, (SLAB - ROWS, CH))
        for chip in range(16):
            even = jnp.concatenate([grads[chip * 72 : chip * 72 + 36, :], tail], axis=0)
            odd = jnp.concatenate([grads[chip * 72 + 36 : chip * 72 + 72, :], tail], axis=0)
            mine[chip, layer] = jnp.where(core == 0, even, odd)
            other[chip, layer] = jnp.where(core == 0, odd, even)


def limits():
    return pltpu.CompilerParams(vmem_limit_bytes=56 * 1024 * 1024)


def run_first(states, weights, bias, guess, gain):
    images = guess.shape[0]
    pair_shape = (images, PAIRS, SIDE, 2 * CH)
    patch_shape = (images, PAIRS + 1, SIDE, 2 * TRIPLE)
    return pl.pallas_call(
        first_kernel,
        out_shape=(
            jax.ShapeDtypeStruct(guess.shape, f32),
            jax.ShapeDtypeStruct((DEPTH, *pair_shape), f32),
            jax.ShapeDtypeStruct((DEPTH, 4 * TRIPLE, 2 * CH), bf16),
        ),
        scratch_shapes=[
            pltpu.VMEM(patch_shape, bf16),
            pltpu.VMEM(patch_shape, bf16),
            pltpu.VMEM((4 * TRIPLE, 2 * CH), bf16),
            pltpu.VMEM(pair_shape, f32),
        ],
        compiler_params=limits(),
        name="first_relaxation",
    )(states, weights, bias, guess, gain)


def run_second(flags, states, guess, begun, slope, adjoint_kernels, scale):
    images = guess.shape[0]
    pair_shape = (images, PAIRS, SIDE, 2 * CH)
    patch_shape = (images, PAIRS + 1, SIDE, 2 * TRIPLE)
    vmem = pl.BlockSpec(memory_space=pltpu.VMEM)
    return pl.pallas_call(
        functools.partial(second_kernel, scale=scale),
        out_shape=(
            jax.ShapeDtypeStruct(guess.shape, f32),
            jax.ShapeDtypeStruct((16, DEPTH, SLAB, CH), f32),
            jax.ShapeDtypeStruct((16, DEPTH, SLAB, CH), f32),
        ),
        in_specs=[pl.BlockSpec(memory_space=pltpu.SMEM)] + [vmem] * 5,
        scratch_shapes=[
            pltpu.VMEM(patch_shape, bf16),
            pltpu.VMEM(pair_shape, f32),
            pltpu.VMEM((TAPS, CH), f32),
            pltpu.VMEM((8, CH), f32),
        ],
        compiler_params=limits(),
        name="second_relaxation",
    )(flags, states, guess, begun, slope, adjoint_kernels)


def scatter_sum(mine, other):
    index = lax.axis_index("dp")
    along_x, along_z = index // 8, (index // 2) % 4
    total = mine + lax.ppermute(other, "dp", [(at, at ^ 1) for at in range(32)])

    def stage(parts, place, shift):
        received = []
        for hop in range(1, 4):
            pairs = [(at, shift(at, hop)) for at in range(32)]
            part = lax.dynamic_index_in_dim(parts, (place + hop) % 4, 0, False)
            received.append(lax.ppermute(part, "dp", pairs))
        return lax.dynamic_index_in_dim(parts, place, 0, False) + received[0] + received[1] + received[2]

    total = total.reshape(4, 4, DEPTH, SLAB, CH)
    total = stage(total, along_x, lambda at, hop: (at // 8 + hop) % 4 * 8 + at % 8)
    return stage(total, along_z, lambda at, hop: at // 8 * 8 + (at // 2 + hop) % 4 * 2 + at % 2)


def per_device(states, weights, bias, guesses, coarse_gain):
    section = lax.axis_index("layer")
    sections = lax.axis_size("layer")
    images = states.shape[1]
    scale = STEP / (images * lax.axis_size("dp"))
    paired = (images, PAIRS, 2, SIDE, CH)
    states = states.reshape(DEPTH, *paired)
    guess = guesses.reshape(paired)
    before = lax.dynamic_slice_in_dim(coarse_gain, jnp.maximum(section - 1, 0), 1, 0)
    inside = (section > 0) & (section < sections - 1)
    before = jnp.where(inside, before, 0.0)
    sent, slope, adjoint_kernels = run_first(states, weights, bias, guess, before)

    parts = lax.all_to_all(sent.reshape(sections, -1, CH), "layer", 0, 0)
    carried = parts[sections - 1]
    begun = [carried, carried]
    for at in range(sections - 2, 0, -1):
        carried = parts[at] + coarse_gain[at - 1] * carried
        begun.append(carried)
    begun = jnp.stack(begun[::-1])
    begun = lax.all_to_all(begun, "layer", 0, 0).reshape(paired)

    flags = jnp.stack([(section == sections - 1).astype(jnp.int32), (lax.axis_index("dp") % 2).astype(jnp.int32)])
    start, mine, other = run_second(flags, states, guess, begun, slope, adjoint_kernels, scale)
    total = scatter_sum(mine, other)
    bias_grad = lax.dynamic_slice_in_dim(total[:, ROWS, :], lax.axis_index("dp") * 4, 4, 1)
    return start.reshape(guesses.shape), total[:, :ROWS, :], bias_grad


def solution(mesh):
    return jax.shard_map(
        per_device,
        mesh=mesh,
        in_specs=(
            P("layer", "dp", None, None, None),
            P("layer", None, None),
            P("layer", None),
            P("layer", "dp", None, None, None),
            P(),
        ),
        out_specs=(P("layer", "dp", None, None, None), P("layer", "dp", None), P("layer", "dp")),
        check_vma=False,
    )
```

time: 569 us -> 116 us (0.20); the launches traced: 559 us -> 114 us
  waiting for transfers between devices: 366 us -> 33.3 us
  blocking collectives: 90.9 us -> 20.2 us
  Pallas kernels: 0 us -> 30.4 us
  matrix products: 26.9 us -> 0 us
  local copies, waits for them, and re-layouts: 27.4 us -> 4.4 us
  other arithmetic: 26.6 us -> 6.14 us
  between operations: 16.5 us -> 0.7 us
  starting transfers between devices: 3.89 us -> 19.2 us
    unnamed x3 -> x0, waiting for transfers between devices: 207 us -> none
    all_gather x1 -> x0, waiting for transfers between devices: 158 us -> none  [prefix_2(): everything = jax.tree.map(lambda part: lax.all_gather(part, axis), shard)]
    unnamed x1 -> x0, blocking collectives: 74.6 us -> none
    pallas_call x0 -> x2, Pallas kernels: none -> 30.4 us  [the longest x1 15.9 us: run_first(): pl.pallas_call(first_kernel, out_shape=(jax.ShapeDtypeStruct(guess.shape,...]
    all_to_all x0 -> x1, blocking collectives: none -> 20.2 us  [per_device(): parts = lax.all_to_all(sent.reshape(sections, -1, CH), 'layer', 0, 0)]
    ppermute x1 -> x7, waiting for transfers between devices: 1.3 us -> 21 us  [the longest x6 18.3 us: stage(): received.append(lax.ppermute(part, 'dp', pairs))]
    select_n x9 -> x0, other arithmetic: 17.4 us -> none  [the longest x8 14.5 us: hop(): return jax.tree.map(lambda a, b: jnp.where(reached, a, b), new, before)]
    all_gather x1 -> x0, blocking collectives: 16.3 us -> none  [prefix_2(): everything = jax.tree.map(lambda part: lax.all_gather(part, axis), shard)]
  transfers between devices with their start and end apart: 3 -> 8, of which waited for: 3 -> 6; matrix products, arithmetic and copies ran while one was open for 5% -> 1% of each run, Pallas kernels for 0% -> 0%
where the time goes in v1:
time: 116 us; the launch traced here: 114 us
  waiting for transfers between devices  33.3 us (29%)
  Pallas kernels  30.4 us (26%)
  blocking collectives  20.2 us (17%)
  starting transfers between devices  19.2 us (17%)
  other arithmetic  6.14 us (5%)
  local copies, waits for them, and re-layouts  4.4 us (4%)
    all_to_all x1, blocking collectives, per_device(): parts = lax.all_to_all(sent.reshape(sections, -1, CH), 'layer', 0, 0)  20.2 us
    ppermute x6, waiting for transfers between devices, stage(): received.append(lax.ppermute(part, 'dp', pairs))  18.3 us
    pallas_call x1, Pallas kernels, run_first(): pl.pallas_call(first_kernel, out_shape=(jax.ShapeDtypeStruct(guess.shape,...  15.9 us
    pallas_call x1, Pallas kernels, run_second(): pl.pallas_call(functools.partial(second_kernel, scale=scale), out_shape=(...  14.6 us
    ppermute x6, starting transfers between devices, stage(): received.append(lax.ppermute(part, 'dp', pairs))  13.8 us
    all_to_all x1, waiting for transfers between devices, per_device(): begun = lax.all_to_all(begun, 'layer', 0, 0).reshape(paired)  12.2 us
    all_to_all x1, starting transfers between devices, per_device(): begun = lax.all_to_all(begun, 'layer', 0, 0).reshape(paired)  5.34 us
    unnamed x8, local copies, waits for them, and re-layouts  3.57 us
  transfers between devices with their start and end apart: 8, of which 6 were waited for; matrix products, arithmetic and copies ran while one was open for 1% of the time, Pallas kernels for 0%

profile of v1, /device:TPU:8, one launch (start us, length us, event | category | flops | bytes accessed | tf_op | source)
XLA Modules:
  0.0 114.3 jit_solution(11791501108108937118)
XLA Ops:
  0.6 1.5 %slice_bitcast_fusion.1 = (f32[128]{0:T(128)S(1)}, f32[128]{0:T(128)S(1)}, f32[128]{0:T(128)S(1)}, f32[128]{0:T(128)S(1)}, f32[128]{0:T(128)S(1)}, /*index=5*/f32[1,128]{1,0:T(1,128)}, f32[128]{0:T(128)S(1)}) fusion(f32[8,128]{1,0:T(8,128)} %param.9, s32[]{:T(128)S(6)} %max.3, pred[]{:T(512)S(6)} %and.48), kind=kLoop, calls=%fused_computation.32 | loop fusion | flops 128 | bytes 7173 | tf_op jit(solution)/shard_map/mul | solution.py:290
  2.1 15.9 %first_relaxation.1 = (f32[2,16,2,32,128]{4,3,2,1,0:T(8,128)}, f32[3,2,16,32,256]{4,3,2,1,0:T(8,128)}, bf16[3,1536,256]{2,1,0:T(8,128)(2,1)}) custom-call(bf16[3,2,16,2,32,128]{5,4,3,2,1,0:T(8,128)(2,1)} %bitcast.48, bf16[3,1152,128]{2,1,0:T(8,128)(2,1)} %weights.1, f32[3,128]{1,0:T(4,128)} %bias.1, f32[2,16,2,32,128]{4,3,2,1,0:T(8,128)} %bitcast.50, ...), custom_call_target="tpu_custom_call" | custom-call | tf_op jit(solution)/shard_map/first_relaxation/pallas_call | solution.py:213
  18.0 20.2 %all_to_all.10 = f32[8,256,128]{2,1,0:T(8,128)S(1)} all-to-all(f32[8,256,128]{2,1,0:T(8,128)} %bitcast.55), channel_id=1, replica_groups=mesh['layer'=8,'dp'=32] {'layer'}, dimensions={0} | all-to-all | bytes 2097152 | tf_op jit(solution)/shard_map/all_to_all | solution.py:286
  38.2 0.7 fusion.2
  38.9 0.7 fusion.5
  39.6 0.7 constant_dynamic-update-slice_fusion.1
  40.3 0.7 fusion.6
  40.9 0.7 constant_dynamic-update-slice_fusion
  41.6 0.7 fusion.7
  42.3 0.7 slice_dynamic-update-slice_fusion
  42.9 0.7 slice_dynamic-update-slice_fusion.1
  43.6 5.3 %all-to-all-start.1 = ((f32[8,256,128]{2,1,0:T(8,128)}), f32[8,256,128]{2,1,0:T(8,128)S(1)}, u32[]{:S(2)}, u32[]{:S(2)}) async-start(f32[8,256,128]{2,1,0:T(8,128)} %slice_dynamic-update-slice_fusion.1), calls=%async_computation.1 | async-start | bytes 2097152 | tf_op jit(solution)/shard_map/all_to_all | solution.py:293
  48.9 0.6 pad_add_fusion.flags
  49.5 12.2 %all-to-all-done.1 = f32[8,256,128]{2,1,0:T(8,128)S(1)} async-done(((f32[8,256,128]{2,1,0:T(8,128)}), f32[8,256,128]{2,1,0:T(8,128)S(1)}, u32[]{:S(2)}, u32[]{:S(2)}) %all-to-all-start.1) | async-done | bytes 1048608 | tf_op jit(solution)/shard_map/all_to_all | solution.py:293
  61.7 1.0 copy-done
  62.7 14.6 %second_relaxation.1 = (f32[2,16,2,32,128]{4,3,2,1,0:T(8,128)}, f32[16,3,40,128]{3,2,1,0:T(8,128)}, f32[16,3,40,128]{3,2,1,0:T(8,128)}) custom-call(s32[2]{0:T(128)} %pad_add_fusion.flags, bf16[3,2,16,2,32,128]{5,4,3,2,1,0:T(8,128)(2,1)} %bitcast.49, f32[2,16,2,32,128]{4,3,2,1,0:T(8,128)} %bitcast.51, f32[2,16,2,32,128]{4,3,2,1,0:T(8,128)} %bitcast.52, ...), custom_call_target="tpu_custom_call" | custom-call | tf_op jit(solution)/shard_map/second_relaxation/pallas_call | solution.py:236
  77.3 2.8 %collective-permute-done = f32[16,3,40,128]{3,2,1,0:T(8,128)S(1)} collective-permute-done((f32[16,3,40,128]{3,2,1,0:T(8,128)}, f32[16,3,40,128]{3,2,1,0:T(8,128)S(1)}, u32[]{:S(2)}, u32[]{:S(2)}) %collective-permute-start) | collective-permute-done | bytes 983072 | tf_op jit(solution)/shard_map/ppermute | solution.py:258
  80.1 1.3 %add.143 = f32[16,3,40,128]{3,2,1,0:T(8,128)S(1)} add(f32[16,3,40,128]{3,2,1,0:T(8,128)} %get-tuple-element.13, f32[16,3,40,128]{3,2,1,0:T(8,128)S(1)} %collective-permute-done) | non-fusion elementwise | flops 245760 | bytes 2949120 | tf_op jit(solution)/shard_map/add | solution.py:258
  81.4 0.1 dynamic-slice_bitcast_fusion.2
  81.4 2.8 %collective-permute-start.3 = (f32[4,3,40,128]{3,2,1,0:T(8,128)S(1)}, f32[4,3,40,128]{3,2,1,0:T(8,128)S(1)}, u32[]{:S(2)}, u32[]{:S(2)}) collective-permute-start(f32[4,3,40,128]{3,2,1,0:T(8,128)S(1)} %get-tuple-element.19), channel_id=1, source_target_pairs={{0,24},{1,25},{2,26},{3,27},{4,28},{5,29},{6,30},{7,31},{8,0},{9,1... | collective-permute-start | bytes 737288 | tf_op jit(solution)/shard_map/ppermute | solution.py:265
  84.3 0.8 collective-permute-start.2
  85.1 0.9 collective-permute-start.1
  86.0 9.1 %collective-permute-done.3 = f32[4,3,40,128]{3,2,1,0:T(8,128)S(1)} collective-permute-done((f32[4,3,40,128]{3,2,1,0:T(8,128)S(1)}, f32[4,3,40,128]{3,2,1,0:T(8,128)S(1)}, u32[]{:S(2)}, u32[]{:S(2)}) %collective-permute-start.3) | collective-permute-done | bytes 245792 | tf_op jit(solution)/shard_map/ppermute | solution.py:265
  95.1 3.7 %collective-permute-done.1 = f32[4,3,40,128]{3,2,1,0:T(8,128)S(1)} collective-permute-done((f32[4,3,40,128]{3,2,1,0:T(8,128)S(1)}, f32[4,3,40,128]{3,2,1,0:T(8,128)S(1)}, u32[]{:S(2)}, u32[]{:S(2)}) %collective-permute-start.1) | collective-permute-done | bytes 245792 | tf_op jit(solution)/shard_map/ppermute | solution.py:265
  98.8 5.5 %collective-permute-start.6 = (f32[3,40,128]{2,1,0:T(8,128)S(1)}, f32[3,40,128]{2,1,0:T(8,128)S(1)}, u32[]{:S(2)}, u32[]{:S(2)}) collective-permute-start(f32[3,40,128]{2,1,0:T(8,128)S(1)} %get-tuple-element.22), channel_id=1, source_target_pairs={{0,6},{1,7},{2,0},{3,1},{4,2},{5,3},{6,4},{7,5},{8,14},{9,15},{10,... | collective-permute-start | bytes 184328 | tf_op jit(solution)/shard_map/ppermute | solution.py:265
  104.3 1.4 %collective-permute-start.5 = (f32[3,40,128]{2,1,0:T(8,128)S(1)}, f32[3,40,128]{2,1,0:T(8,128)S(1)}, u32[]{:S(2)}, u32[]{:S(2)}) collective-permute-start(f32[3,40,128]{2,1,0:T(8,128)S(1)} %get-tuple-element.23), channel_id=1, source_target_pairs={{0,4},{1,5},{2,6},{3,7},{4,0},{5,1},{6,2},{7,3},{8,12},{9,13},{10,... | collective-permute-start | bytes 184328 | tf_op jit(solution)/shard_map/ppermute | solution.py:265
  105.8 2.4 %collective-permute-start.4 = (f32[3,40,128]{2,1,0:T(8,128)S(1)}, f32[3,40,128]{2,1,0:T(8,128)S(1)}, u32[]{:S(2)}, u32[]{:S(2)}) collective-permute-start(f32[3,40,128]{2,1,0:T(8,128)S(1)} %get-tuple-element.21), channel_id=1, source_target_pairs={{0,2},{1,3},{2,4},{3,5},{4,6},{5,7},{6,0},{7,1},{8,10},{9,11},{10,... | collective-permute-start | bytes 184328 | tf_op jit(solution)/shard_map/ppermute | solution.py:265
  108.1 1.2 %collective-permute-done.6 = f32[3,40,128]{2,1,0:T(8,128)S(1)} collective-permute-done((f32[3,40,128]{2,1,0:T(8,128)S(1)}, f32[3,40,128]{2,1,0:T(8,128)S(1)}, u32[]{:S(2)}, u32[]{:S(2)}) %collective-permute-start.6) | collective-permute-done | bytes 61472 | tf_op jit(solution)/shard_map/ppermute | solution.py:265
  109.3 4.2 %collective-permute-done.5 = f32[3,40,128]{2,1,0:T(8,128)S(1)} collective-permute-done((f32[3,40,128]{2,1,0:T(8,128)S(1)}, f32[3,40,128]{2,1,0:T(8,128)S(1)}, u32[]{:S(2)}, u32[]{:S(2)}) %collective-permute-start.5) | collective-permute-done | bytes 61472 | tf_op jit(solution)/shard_map/ppermute | solution.py:265
  113.6 0.0 copy-start.1
  113.6 0.1 constant_dynamic-slice_fusion
  113.7 0.6 copy.10
  (9 shorter events, 0.1 us)
Async XLA Ops:
  43.6 18.1 %all-to-all-start.1 = ((f32[8,256,128]{2,1,0:T(8,128)}), f32[8,256,128]{2,1,0:T(8,128)S(1)}, u32[]{:S(2)}, u32[]{:S(2)}) async-start(f32[8,256,128]{2,1,0:T(8,128)} %slice_dynamic-update-slice_fusion.1), calls=%async_computation.1 | async-start | bytes 2097152 | tf_op jit(solution)/shard_map/all_to_all | solution.py:293
  61.7 1.0 copy-start
  77.3 2.8 %collective-permute-start = (f32[16,3,40,128]{3,2,1,0:T(8,128)}, f32[16,3,40,128]{3,2,1,0:T(8,128)S(1)}, u32[]{:S(2)}, u32[]{:S(2)}) collective-permute-start(f32[16,3,40,128]{3,2,1,0:T(8,128)} %get-tuple-element.14), channel_id=1, source_target_pairs={{0,1},{1,0},{2,3},{3,2},{4,5},{5,4},{6,7},{7,6},{8,9},{9,8},{10,11... | collective-permute-start | bytes 2949128 | tf_op jit(solution)/shard_map/ppermute | solution.py:258
  81.4 13.7 %collective-permute-start.3 = (f32[4,3,40,128]{3,2,1,0:T(8,128)S(1)}, f32[4,3,40,128]{3,2,1,0:T(8,128)S(1)}, u32[]{:S(2)}, u32[]{:S(2)}) collective-permute-start(f32[4,3,40,128]{3,2,1,0:T(8,128)S(1)} %get-tuple-element.19), channel_id=1, source_target_pairs={{0,24},{1,25},{2,26},{3,27},{4,28},{5,29},{6,30},{7,31},{8,0},{9,1... | collective-permute-start | bytes 737288 | tf_op jit(solution)/shard_map/ppermute | solution.py:265
  84.3 10.8 %collective-permute-start.2 = (f32[4,3,40,128]{3,2,1,0:T(8,128)S(1)}, f32[4,3,40,128]{3,2,1,0:T(8,128)S(1)}, u32[]{:S(2)}, u32[]{:S(2)}) collective-permute-start(f32[4,3,40,128]{3,2,1,0:T(8,128)S(1)} %get-tuple-element.20), channel_id=1, source_target_pairs={{0,16},{1,17},{2,18},{3,19},{4,20},{5,21},{6,22},{7,23},{8,24},{9,... | collective-permute-start | bytes 737288 | tf_op jit(solution)/shard_map/ppermute | solution.py:265
  85.1 13.7 %collective-permute-start.1 = (f32[4,3,40,128]{3,2,1,0:T(8,128)S(1)}, f32[4,3,40,128]{3,2,1,0:T(8,128)S(1)}, u32[]{:S(2)}, u32[]{:S(2)}) collective-permute-start(f32[4,3,40,128]{3,2,1,0:T(8,128)S(1)} %get-tuple-element.18), channel_id=1, source_target_pairs={{0,8},{1,9},{2,10},{3,11},{4,12},{5,13},{6,14},{7,15},{8,16},{9,17... | collective-permute-start | bytes 737288 | tf_op jit(solution)/shard_map/ppermute | solution.py:265
  98.8 10.5 %collective-permute-start.6 = (f32[3,40,128]{2,1,0:T(8,128)S(1)}, f32[3,40,128]{2,1,0:T(8,128)S(1)}, u32[]{:S(2)}, u32[]{:S(2)}) collective-permute-start(f32[3,40,128]{2,1,0:T(8,128)S(1)} %get-tuple-element.22), channel_id=1, source_target_pairs={{0,6},{1,7},{2,0},{3,1},{4,2},{5,3},{6,4},{7,5},{8,14},{9,15},{10,... | collective-permute-start | bytes 184328 | tf_op jit(solution)/shard_map/ppermute | solution.py:265
  104.3 9.3 %collective-permute-start.5 = (f32[3,40,128]{2,1,0:T(8,128)S(1)}, f32[3,40,128]{2,1,0:T(8,128)S(1)}, u32[]{:S(2)}, u32[]{:S(2)}) collective-permute-start(f32[3,40,128]{2,1,0:T(8,128)S(1)} %get-tuple-element.23), channel_id=1, source_target_pairs={{0,4},{1,5},{2,6},{3,7},{4,0},{5,1},{6,2},{7,3},{8,12},{9,13},{10,... | collective-permute-start | bytes 184328 | tf_op jit(solution)/shard_map/ppermute | solution.py:265
  105.8 7.8 %collective-permute-start.4 = (f32[3,40,128]{2,1,0:T(8,128)S(1)}, f32[3,40,128]{2,1,0:T(8,128)S(1)}, u32[]{:S(2)}, u32[]{:S(2)}) collective-permute-start(f32[3,40,128]{2,1,0:T(8,128)S(1)} %get-tuple-element.21), channel_id=1, source_target_pairs={{0,2},{1,3},{2,4},{3,5},{4,6},{5,7},{6,0},{7,1},{8,10},{9,11},{10,... | collective-permute-start | bytes 184328 | tf_op jit(solution)/shard_map/ppermute | solution.py:265
  113.6 0.7 copy-start.1

commit v2 on v1

v2 whole, which is shorter than its diff:
```python
import functools

import jax
import jax.numpy as jnp
from jax import lax
from jax.experimental import pallas as pl
from jax.experimental.pallas import tpu as pltpu
from jax.sharding import PartitionSpec as P

CH = 128
SIDE = 32
PAIRS = SIDE // 2
DEPTH = 3
TAPS = 9 * CH
TRIPLE = 3 * CH
STEP = 0.5
BLOCK = PAIRS
FINE = 4
ROWS = 36
SLAB = 40
f32 = jnp.float32
bf16 = jnp.bfloat16


def dot(a, b):
    return jnp.dot(a, b, preferred_element_type=f32)


def for_steps(images, body):
    steps = PAIRS // FINE

    def one(at, carry):
        body(at // steps, (at % steps) * FINE)
        return carry

    lax.fori_loop(0, images * steps, one, 0)


def clear_edges(ref):
    images = ref.shape[0]
    zero = jnp.zeros((images, 1, SIDE, TRIPLE), bf16)
    ref[:, 0:1, :, 0:TRIPLE] = zero
    ref[:, PAIRS : PAIRS + 1, :, TRIPLE:] = zero


def spread(ref, image, pair, half, value):
    rows = value.shape[0]
    column = lax.broadcasted_iota(jnp.int32, value.shape, 0) & (SIDE - 1)
    left = jnp.where(column == 0, 0.0, pltpu.roll(value, 1, 0))
    right = jnp.where(column == SIDE - 1, 0.0, pltpu.roll(value, rows - 1, 0))
    base = (1 - half) * TRIPLE
    for at, part in enumerate((left, value, right)):
        lanes = slice(base + at * CH, base + (at + 1) * CH)
        ref[image, pl.ds(pair + half, rows // SIDE), :, lanes] = part.astype(bf16).reshape(-1, SIDE, CH)


def convolve(ref, image, pair, kernel):
    upper = ref[image, pl.ds(pair, BLOCK)].reshape(BLOCK * SIDE, 2 * TRIPLE)
    lower = ref[image, pl.ds(pair + 1, BLOCK)].reshape(BLOCK * SIDE, 2 * TRIPLE)
    top, middle, bottom = (kernel[at * TRIPLE : (at + 1) * TRIPLE, :] for at in range(3))
    zero = jnp.zeros((TRIPLE, CH), bf16)

    def beside(left, right):
        return jnp.concatenate([jnp.concatenate(left, axis=0), jnp.concatenate(right, axis=0)], axis=1)

    return dot(upper, beside((top, middle), (zero, top))) + dot(lower, beside((bottom, zero), (middle, bottom)))


def gather(states, field, layer, image, pair, count):
    for half in range(2):
        value = states[layer, image, pl.ds(pair, count), half].reshape(count * SIDE, CH)
        spread(field, image, pair, half, value.astype(f32))


def first_kernel(
    states_from, weights_from, bias, guess_from, gain, flags,
    sent, slope_to, turned_to,
    states, weights, guess, slope, turned, field, patches, adjoint, came, left,
):
    images = guess.shape[0]
    arrivals = {}
    for layer in reversed(range(DEPTH)):
        arrivals[layer] = [
            pltpu.make_async_copy(states_from.at[layer], states.at[layer], came.at[layer]),
            pltpu.make_async_copy(weights_from.at[layer], weights.at[layer], came.at[DEPTH + layer]),
        ]
        for copy in arrivals[layer]:
            copy.start()
        if layer == DEPTH - 1:
            guess_copy = pltpu.make_async_copy(guess_from, guess, came.at[2 * DEPTH])
            guess_copy.start()
    departures = []
    clear_edges(field)
    clear_edges(patches)
    section, sections = flags[0], flags[1]
    inside = (section > 0) & (section < sections - 1)
    before = jnp.where(inside, gain[pl.ds(jnp.maximum(section - 1, 0), 1), :], 0.0).reshape(1, 1, CH)
    for layer in reversed(range(DEPTH)):
        last = layer == DEPTH - 1
        if last:
            for copy in arrivals[layer]:
                copy.wait()
            for_steps(images, lambda image, pair: gather(states, field, layer, image, pair, FINE))
        for tap in range(9):
            source = (8 - tap) * CH
            turned[layer, tap * CH : (tap + 1) * CH, :] = weights[layer, source : source + CH, :].T
        copy = pltpu.make_async_copy(turned.at[layer], turned_to.at[layer], left.at[DEPTH + layer])
        copy.start()
        departures.append(copy)
        if last:
            guess_copy.wait()
        offset = bias[layer : layer + 1, :]
        for image in range(images):
            both = convolve(field, image, 0, weights.at[layer])
            for half in range(2):
                lanes = slice(half * CH, (half + 1) * CH)
                value = jnp.tanh(both[:, lanes] + offset)
                value = 1.0 - value * value
                slope[layer, image, :, :, lanes] = value.reshape(PAIRS, SIDE, CH)
                now = guess[image, :, half] if last else adjoint[image, :, :, lanes]
                spread(patches, image, 0, half, value * now.reshape(PAIRS * SIDE, CH))
        copy = pltpu.make_async_copy(slope.at[layer], slope_to.at[layer], left.at[layer])
        copy.start()
        departures.append(copy)
        if layer:
            for copy in arrivals[layer - 1]:
                copy.wait()
        for image in range(images):
            both = convolve(patches, image, 0, turned.at[layer])
            for half in range(2):
                lanes = slice(half * CH, (half + 1) * CH)
                change = STEP * both[:, lanes].reshape(PAIRS, SIDE, CH)
                now = guess[image, :, half] if last else adjoint[image, :, :, lanes]
                if layer:
                    adjoint[image, :, :, lanes] = now + change
                else:
                    sent[image, :, half] = now + change - before * guess[image, :, half]
            if layer:
                gather(states, field, layer - 1, image, 0, PAIRS)
    for copy in departures:
        copy.wait()


def second_kernel(
    states_from, guess_from, begun, slope_from, turned_from, flags,
    start, mine, other,
    states, guess, slope, turned, patches, adjoint, grads, sums, came, scale,
):
    images = guess.shape[0]
    arrivals = {}
    for layer in reversed(range(DEPTH)):
        arrivals[layer] = [
            pltpu.make_async_copy(source.at[layer], to.at[layer], came.at[at * DEPTH + layer])
            for at, (source, to) in enumerate(((slope_from, slope), (turned_from, turned), (states_from, states)))
        ]
    guess_copy = pltpu.make_async_copy(guess_from, guess, came.at[3 * DEPTH])
    guess_copy.start()
    for layer in reversed(range(DEPTH)):
        for copy in arrivals[layer]:
            copy.start()
    clear_edges(patches)
    last = flags[0] == flags[1] - 1
    core = flags[2]
    guess_copy.wait()
    for layer in reversed(range(DEPTH)):
        sums[...] = jnp.zeros_like(sums)
        arrivals[layer][0].wait()

        def derive(image, pair):
            for half in range(2):
                lanes = slice(half * CH, (half + 1) * CH)
                if layer == DEPTH - 1:
                    now = jnp.where(
                        last, guess[image, pl.ds(pair, FINE), half], begun[image, pl.ds(pair, FINE), half]
                    )
                    adjoint[image, pl.ds(pair, FINE), :, lanes] = now
                else:
                    now = adjoint[image, pl.ds(pair, FINE), :, lanes]
                value = slope[layer, image, pl.ds(pair, FINE), :, lanes] * now
                value = value.reshape(FINE * SIDE, CH).astype(bf16).astype(f32)
                sums[...] += value.reshape(-1, 8, CH).sum(axis=0)
                spread(patches, image, pair, half, value)

        for_steps(images, derive)
        arrivals[layer][1].wait()
        for image in range(images):
            both = convolve(patches, image, 0, turned.at[layer])
            for half in range(2):
                lanes = slice(half * CH, (half + 1) * CH)
                change = STEP * both[:, lanes].reshape(PAIRS, SIDE, CH)
                now = adjoint[image, :, :, lanes]
                if layer:
                    adjoint[image, :, :, lanes] = now + change
                else:
                    start[image, :, half] = now + change
        arrivals[layer][2].wait()

        points = images * PAIRS * SIDE
        halves = [states[layer, :, :, half].reshape(points, CH) for half in range(2)]
        field = jnp.concatenate(halves, axis=1)
        for group in range(2):
            for third in range(3):
                lanes = slice(third * 2 * CH, (third + 1) * 2 * CH)
                part = patches[:, group : group + PAIRS, :, lanes].reshape(points, 2 * CH)
                result = lax.dot_general(field, part, (((0,), (0,)), ((), ())), preferred_element_type=f32)
                for piece in range(2):
                    row, side = divmod(third * 2 + piece, 3)
                    for half in range(2):
                        tap = row + 2 * group - half
                        if not 0 <= tap <= 2:
                            continue
                        block = ((2 - tap) * 3 + 2 - side) * CH
                        value = result[half * CH : (half + 1) * CH, piece * CH : (piece + 1) * CH] * scale
                        if (group, row, half) in ((0, 0, 0), (0, 1, 0), (1, 0, 0)):
                            grads[block : block + CH, :] = value
                        else:
                            grads[block : block + CH, :] += value
        total = scale * jnp.sum(sums[...], axis=0, keepdims=True)
        tail = jnp.broadcast_to(total, (SLAB - ROWS, CH))
        for chip in range(16):
            even = jnp.concatenate([grads[chip * 72 : chip * 72 + 36, :], tail], axis=0)
            odd = jnp.concatenate([grads[chip * 72 + 36 : chip * 72 + 72, :], tail], axis=0)
            mine[chip, layer] = jnp.where(core == 0, even, odd)
            other[chip, layer] = jnp.where(core == 0, odd, even)


def middle_kernel(parts, gain, begun):
    count = parts.shape[0]
    carried = parts[count - 1]
    begun[count - 1] = carried
    begun[count - 2] = carried
    for at in range(count - 2, 0, -1):
        carried = parts[at] + gain[at - 1 : at, :] * carried
        begun[at - 1] = carried


ANY = pl.BlockSpec(memory_space=pltpu.HBM)
VMEM = pl.BlockSpec(memory_space=pltpu.VMEM)
SMEM = pl.BlockSpec(memory_space=pltpu.SMEM)


def limits(mib):
    return pltpu.CompilerParams(vmem_limit_bytes=mib * 1024 * 1024)


def run_first(states, weights, bias, guess, gain, flags):
    images = guess.shape[0]
    pair_shape = (images, PAIRS, SIDE, 2 * CH)
    patch_shape = (images, PAIRS + 1, SIDE, 2 * TRIPLE)
    slope = (DEPTH, *pair_shape)
    return pl.pallas_call(
        first_kernel,
        out_shape=(
            jax.ShapeDtypeStruct(guess.shape, f32),
            jax.ShapeDtypeStruct(slope, f32),
            jax.ShapeDtypeStruct(weights.shape, bf16),
        ),
        in_specs=[ANY, ANY, VMEM, ANY, VMEM, SMEM],
        out_specs=(VMEM, ANY, ANY),
        scratch_shapes=[
            pltpu.VMEM(states.shape, bf16),
            pltpu.VMEM(weights.shape, bf16),
            pltpu.VMEM(guess.shape, f32),
            pltpu.VMEM(slope, f32),
            pltpu.VMEM(weights.shape, bf16),
            pltpu.VMEM(patch_shape, bf16),
            pltpu.VMEM(patch_shape, bf16),
            pltpu.VMEM(pair_shape, f32),
            pltpu.SemaphoreType.DMA((2 * DEPTH + 1,)),
            pltpu.SemaphoreType.DMA((2 * DEPTH,)),
        ],
        compiler_params=limits(60),
        name="first_relaxation",
    )(states, weights, bias, guess, gain, flags)


def run_middle(parts, gain):
    return pl.pallas_call(
        middle_kernel,
        out_shape=jax.ShapeDtypeStruct(parts.shape, f32),
        in_specs=[VMEM, VMEM],
        out_specs=VMEM,
        name="recurrence",
    )(parts, gain)


def run_second(states, guess, begun, slope, turned, flags, scale):
    images = guess.shape[0]
    pair_shape = (images, PAIRS, SIDE, 2 * CH)
    patch_shape = (images, PAIRS + 1, SIDE, 2 * TRIPLE)
    slabs = jax.ShapeDtypeStruct((16, DEPTH, SLAB, CH), f32)
    return pl.pallas_call(
        functools.partial(second_kernel, scale=scale),
        out_shape=(jax.ShapeDtypeStruct(guess.shape, f32), slabs, slabs),
        in_specs=[ANY, ANY, VMEM, ANY, ANY, SMEM],
        out_specs=(VMEM, VMEM, VMEM),
        scratch_shapes=[
            pltpu.VMEM(states.shape, bf16),
            pltpu.VMEM(guess.shape, f32),
            pltpu.VMEM(slope.shape, f32),
            pltpu.VMEM(turned.shape, bf16),
            pltpu.VMEM(patch_shape, bf16),
            pltpu.VMEM(pair_shape, f32),
            pltpu.VMEM((TAPS, CH), f32),
            pltpu.VMEM((8, CH), f32),
            pltpu.SemaphoreType.DMA((3 * DEPTH + 1,)),
        ],
        compiler_params=limits(60),
        name="second_relaxation",
    )(states, guess, begun, slope, turned, flags)


def scatter_sum(mine, other):
    index = lax.axis_index("dp")
    along_x, along_z = index // 8, (index // 2) % 4
    total = mine + lax.ppermute(other, "dp", [(at, at ^ 1) for at in range(32)])

    def stage(parts, place, shift):
        received = []
        for hop in range(1, 4):
            pairs = [(at, shift(at, hop)) for at in range(32)]
            part = lax.dynamic_index_in_dim(parts, (place + hop) % 4, 0, False)
            received.append(lax.ppermute(part, "dp", pairs))
        return lax.dynamic_index_in_dim(parts, place, 0, False) + received[0] + received[1] + received[2]

    total = total.reshape(4, 4, DEPTH, SLAB, CH)
    total = stage(total, along_x, lambda at, hop: (at // 8 + hop) % 4 * 8 + at % 8)
    return stage(total, along_z, lambda at, hop: at // 8 * 8 + (at // 2 + hop) % 4 * 2 + at % 2)


def per_device(states, weights, bias, guesses, coarse_gain):
    section = lax.axis_index("layer")
    sections = lax.axis_size("layer")
    images = states.shape[1]
    scale = STEP / (images * lax.axis_size("dp"))
    paired = (images, PAIRS, 2, SIDE, CH)
    states = states.reshape(DEPTH, *paired)
    guess = guesses.reshape(paired)
    flags = jnp.stack([section, jnp.int32(sections), lax.axis_index("dp") % 2]).astype(jnp.int32)
    sent, slope, turned = run_first(states, weights, bias, guess, coarse_gain, flags)

    parts = lax.all_to_all(sent.reshape(sections, -1, CH), "layer", 0, 0)
    begun = run_middle(parts, coarse_gain)
    begun = lax.all_to_all(begun, "layer", 0, 0).reshape(paired)

    start, mine, other = run_second(states, guess, begun, slope, turned, flags, scale)
    total = scatter_sum(mine, other)
    bias_grad = lax.dynamic_slice_in_dim(total[:, ROWS, :], lax.axis_index("dp") * 4, 4, 1)
    return start.reshape(guesses.shape), total[:, :ROWS, :], bias_grad


def solution(mesh):
    return jax.shard_map(
        per_device,
        mesh=mesh,
        in_specs=(
            P("layer", "dp", None, None, None),
            P("layer", None, None),
            P("layer", None),
            P("layer", "dp", None, None, None),
            P(),
        ),
        out_specs=(P("layer", "dp", None, None, None), P("layer", "dp", None), P("layer", "dp")),
        check_vma=False,
    )
```

time: 116 us -> 105 us (0.905)
  blocking collectives: 20.2 us -> 39.5 us
  waiting for transfers between devices: 33.3 us -> 21 us
  starting transfers between devices: 19.2 us -> 13.9 us
  Pallas kernels: 30.4 us -> 25.1 us
  other arithmetic: 6.14 us -> 1.99 us
  local copies, waits for them, and re-layouts: 4.4 us -> 0.76 us
    all_to_all x0 -> x1, blocking collectives: none -> 19.2 us  [per_device(): begun = lax.all_to_all(begun, 'layer', 0, 0).reshape(paired)]
    all_to_all x1 -> x0, waiting for transfers between devices: 12.2 us -> none  [per_device(): begun = lax.all_to_all(begun, 'layer', 0, 0).reshape(paired)]
    all_to_all x1 -> x0, starting transfers between devices: 5.34 us -> none  [per_device(): begun = lax.all_to_all(begun, 'layer', 0, 0).reshape(paired)]
    pallas_call x1, Pallas kernels: 15.9 us -> 10.8 us  [run_first(): pl.pallas_call(first_kernel, out_shape=(jax.ShapeDtypeStruct(guess.shape,...]
    unnamed x8 -> x3, local copies, waits for them, and re-layouts: 3.57 us -> 0.59 us
    unnamed x4 -> x0, other arithmetic: 2.73 us -> none
    pallas_call x1, Pallas kernels: 14.6 us -> 12 us  [run_second(): pl.pallas_call(functools.partial(second_kernel, scale=scale), out_shape=(...]
    pallas_call x0 -> x1, Pallas kernels: none -> 2.27 us  [run_middle(): pl.pallas_call(middle_kernel, out_shape=jax.ShapeDtypeStruct(parts.shape,...]
  transfers between devices with their start and end apart: 8 -> 7, of which waited for: 6 -> 5; matrix products, arithmetic and copies ran while one was open for 1% -> 0% of each run, Pallas kernels for 0% -> 0%
where the time goes in v2:
time: 105 us; the launch traced here: 103 us
  blocking collectives  39.5 us (38%)
  Pallas kernels  25.1 us (24%)
  waiting for transfers between devices  21 us (20%)
  starting transfers between devices  13.9 us (13%)
  other arithmetic  1.99 us (2%)
    all_to_all x1, blocking collectives, per_device(): parts = lax.all_to_all(sent.reshape(sections, -1, CH), 'layer', 0, 0)  20.3 us
    all_to_all x1, blocking collectives, per_device(): begun = lax.all_to_all(begun, 'layer', 0, 0).reshape(paired)  19.2 us
    ppermute x6, waiting for transfers between devices, stage(): received.append(lax.ppermute(part, 'dp', pairs))  18.3 us
    ppermute x6, starting transfers between devices, stage(): received.append(lax.ppermute(part, 'dp', pairs))  13.8 us
    pallas_call x1, Pallas kernels, run_second(): pl.pallas_call(functools.partial(second_kernel, scale=scale), out_shape=(...  12 us
    pallas_call x1, Pallas kernels, run_first(): pl.pallas_call(first_kernel, out_shape=(jax.ShapeDtypeStruct(guess.shape,...  10.8 us
    ppermute x1, waiting for transfers between devices, scatter_sum(): total = mine + lax.ppermute(other, 'dp', [(at, at ^ 1) for at in range(32)])  2.69 us
    pallas_call x1, Pallas kernels, run_middle(): pl.pallas_call(middle_kernel, out_shape=jax.ShapeDtypeStruct(parts.shape,...  2.27 us
  transfers between devices with their start and end apart: 7, of which 5 were waited for; matrix products, arithmetic and copies ran while one was open for 0% of the time, Pallas kernels for 0%

profile of v2, /device:TPU:8, one launch (start us, length us, event | category | flops | bytes accessed | tf_op | source)
XLA Modules:
  0.0 103.0 jit_solution(2506614663661285774)
XLA Ops:
  0.6 0.6 pad_add_fusion.flags
  1.3 10.8 %first_relaxation.1 = (f32[2,16,2,32,128]{4,3,2,1,0:T(8,128)}, f32[3,2,16,32,256]{4,3,2,1,0:T(8,128)}, bf16[3,1152,128]{2,1,0:T(8,128)(2,1)}) custom-call(bf16[3,2,16,2,32,128]{5,4,3,2,1,0:T(8,128)(2,1)} %bitcast.36, bf16[3,1152,128]{2,1,0:T(8,128)(2,1)} %weights_from.1, f32[3,128]{1,0:T(4,128)} %bias.1, f32[2,16,2,32,128]{4,3,2,1,0:T(8,128)} %bitcast.39, ...), custom_call_target="tpu_custom_call" | custom-call | tf_op jit(solution)/shard_map/first_relaxation/pallas_call | solution.py:251
  12.1 20.3 %all_to_all.10.parts = f32[8,256,128]{2,1,0:T(8,128)} all-to-all(f32[8,256,128]{2,1,0:T(8,128)} %bitcast.43), channel_id=1, replica_groups=mesh['layer'=8,'dp'=32] {'layer'}, dimensions={0} | all-to-all | bytes 2097152 | tf_op jit(solution)/shard_map/all_to_all | solution.py:342
  32.4 2.3 %recurrence.1 = f32[8,256,128]{2,1,0:T(8,128)} custom-call(f32[8,256,128]{2,1,0:T(8,128)} %all_to_all.10.parts, f32[8,128]{1,0:T(8,128)} %gain.3), custom_call_target="tpu_custom_call" | custom-call | tf_op jit(solution)/shard_map/recurrence/pallas_call | solution.py:278
  34.7 19.2 %all_to_all.11 = f32[8,256,128]{2,1,0:T(8,128)} all-to-all(f32[8,256,128]{2,1,0:T(8,128)} %recurrence.1), channel_id=1, replica_groups=mesh['layer'=8,'dp'=32] {'layer'}, dimensions={0} | all-to-all | bytes 2097152 | tf_op jit(solution)/shard_map/all_to_all | solution.py:344
  53.8 12.0 %second_relaxation.1 = (f32[2,16,2,32,128]{4,3,2,1,0:T(8,128)}, f32[16,3,40,128]{3,2,1,0:T(8,128)}, f32[16,3,40,128]{3,2,1,0:T(8,128)}) custom-call(bf16[3,2,16,2,32,128]{5,4,3,2,1,0:T(8,128)(2,1)} %bitcast.37, f32[2,16,2,32,128]{4,3,2,1,0:T(8,128)} %bitcast.40, f32[2,16,2,32,128]{4,3,2,1,0:T(8,128)} %bitcast.38, ...), custom_call_target="tpu_custom_call" | custom-call | tf_op jit(solution)/shard_map/second_relaxation/pallas_call | solution.py:292
  65.9 0.1 collective-permute-start
  66.0 2.7 %collective-permute-done = f32[16,3,40,128]{3,2,1,0:T(8,128)S(1)} collective-permute-done((f32[16,3,40,128]{3,2,1,0:T(8,128)}, f32[16,3,40,128]{3,2,1,0:T(8,128)S(1)}, u32[]{:S(2)}, u32[]{:S(2)}) %collective-permute-start) | collective-permute-done | bytes 983072 | tf_op jit(solution)/shard_map/ppermute | solution.py:316
  68.7 1.3 %add.96 = f32[16,3,40,128]{3,2,1,0:T(8,128)S(1)} add(f32[16,3,40,128]{3,2,1,0:T(8,128)} %get-tuple-element.13, f32[16,3,40,128]{3,2,1,0:T(8,128)S(1)} %collective-permute-done) | non-fusion elementwise | flops 245760 | bytes 2949120 | tf_op jit(solution)/shard_map/add | solution.py:316
  70.0 0.1 dynamic-slice_bitcast_fusion.2
  70.1 2.8 %collective-permute-start.3 = (f32[4,3,40,128]{3,2,1,0:T(8,128)S(1)}, f32[4,3,40,128]{3,2,1,0:T(8,128)S(1)}, u32[]{:S(2)}, u32[]{:S(2)}) collective-permute-start(f32[4,3,40,128]{3,2,1,0:T(8,128)S(1)} %get-tuple-element.16), channel_id=1, source_target_pairs={{0,24},{1,25},{2,26},{3,27},{4,28},{5,29},{6,30},{7,31},{8,0},{9,1... | collective-permute-start | bytes 737288 | tf_op jit(solution)/shard_map/ppermute | solution.py:323
  72.9 0.8 collective-permute-start.2
  73.7 0.9 collective-permute-start.1
  74.6 9.1 %collective-permute-done.3 = f32[4,3,40,128]{3,2,1,0:T(8,128)S(1)} collective-permute-done((f32[4,3,40,128]{3,2,1,0:T(8,128)S(1)}, f32[4,3,40,128]{3,2,1,0:T(8,128)S(1)}, u32[]{:S(2)}, u32[]{:S(2)}) %collective-permute-start.3) | collective-permute-done | bytes 245792 | tf_op jit(solution)/shard_map/ppermute | solution.py:323
  83.7 0.0 collective-permute-done.2
  83.7 3.7 %collective-permute-done.1 = f32[4,3,40,128]{3,2,1,0:T(8,128)S(1)} collective-permute-done((f32[4,3,40,128]{3,2,1,0:T(8,128)S(1)}, f32[4,3,40,128]{3,2,1,0:T(8,128)S(1)}, u32[]{:S(2)}, u32[]{:S(2)}) %collective-permute-start.1) | collective-permute-done | bytes 245792 | tf_op jit(solution)/shard_map/ppermute | solution.py:323
  87.5 5.5 %collective-permute-start.6 = (f32[3,40,128]{2,1,0:T(8,128)S(1)}, f32[3,40,128]{2,1,0:T(8,128)S(1)}, u32[]{:S(2)}, u32[]{:S(2)}) collective-permute-start(f32[3,40,128]{2,1,0:T(8,128)S(1)} %get-tuple-element.19), channel_id=1, source_target_pairs={{0,6},{1,7},{2,0},{3,1},{4,2},{5,3},{6,4},{7,5},{8,14},{9,15},{10,... | collective-permute-start | bytes 184328 | tf_op jit(solution)/shard_map/ppermute | solution.py:323
  93.0 1.4 %collective-permute-start.5 = (f32[3,40,128]{2,1,0:T(8,128)S(1)}, f32[3,40,128]{2,1,0:T(8,128)S(1)}, u32[]{:S(2)}, u32[]{:S(2)}) collective-permute-start(f32[3,40,128]{2,1,0:T(8,128)S(1)} %get-tuple-element.20), channel_id=1, source_target_pairs={{0,4},{1,5},{2,6},{3,7},{4,0},{5,1},{6,2},{7,3},{8,12},{9,13},{10,... | collective-permute-start | bytes 184328 | tf_op jit(solution)/shard_map/ppermute | solution.py:323
  94.4 2.4 %collective-permute-start.4 = (f32[3,40,128]{2,1,0:T(8,128)S(1)}, f32[3,40,128]{2,1,0:T(8,128)S(1)}, u32[]{:S(2)}, u32[]{:S(2)}) collective-permute-start(f32[3,40,128]{2,1,0:T(8,128)S(1)} %get-tuple-element.18), channel_id=1, source_target_pairs={{0,2},{1,3},{2,4},{3,5},{4,6},{5,7},{6,0},{7,1},{8,10},{9,11},{10,... | collective-permute-start | bytes 184328 | tf_op jit(solution)/shard_map/ppermute | solution.py:323
  96.8 1.0 collective-permute-done.6
  97.7 4.5 %collective-permute-done.5 = f32[3,40,128]{2,1,0:T(8,128)S(1)} collective-permute-done((f32[3,40,128]{2,1,0:T(8,128)S(1)}, f32[3,40,128]{2,1,0:T(8,128)S(1)}, u32[]{:S(2)}, u32[]{:S(2)}) %collective-permute-start.5) | collective-permute-done | bytes 61472 | tf_op jit(solution)/shard_map/ppermute | solution.py:323
  102.3 0.0 collective-permute-done.4
  102.3 0.0 copy-start
  102.3 0.1 constant_dynamic-slice_fusion
  102.4 0.6 copy.10
  103.0 0.0 copy-done
  (4 shorter events, 0.1 us)
Async XLA Ops:
  65.9 2.9 %collective-permute-start = (f32[16,3,40,128]{3,2,1,0:T(8,128)}, f32[16,3,40,128]{3,2,1,0:T(8,128)S(1)}, u32[]{:S(2)}, u32[]{:S(2)}) collective-permute-start(f32[16,3,40,128]{3,2,1,0:T(8,128)} %get-tuple-element.14), channel_id=1, source_target_pairs={{0,1},{1,0},{2,3},{3,2},{4,5},{5,4},{6,7},{7,6},{8,9},{9,8},{10,11... | collective-permute-start | bytes 2949128 | tf_op jit(solution)/shard_map/ppermute | solution.py:316
  70.1 13.6 %collective-permute-start.3 = (f32[4,3,40,128]{3,2,1,0:T(8,128)S(1)}, f32[4,3,40,128]{3,2,1,0:T(8,128)S(1)}, u32[]{:S(2)}, u32[]{:S(2)}) collective-permute-start(f32[4,3,40,128]{3,2,1,0:T(8,128)S(1)} %get-tuple-element.16), channel_id=1, source_target_pairs={{0,24},{1,25},{2,26},{3,27},{4,28},{5,29},{6,30},{7,31},{8,0},{9,1... | collective-permute-start | bytes 737288 | tf_op jit(solution)/shard_map/ppermute | solution.py:323
  72.9 10.8 %collective-permute-start.2 = (f32[4,3,40,128]{3,2,1,0:T(8,128)S(1)}, f32[4,3,40,128]{3,2,1,0:T(8,128)S(1)}, u32[]{:S(2)}, u32[]{:S(2)}) collective-permute-start(f32[4,3,40,128]{3,2,1,0:T(8,128)S(1)} %get-tuple-element.17), channel_id=1, source_target_pairs={{0,16},{1,17},{2,18},{3,19},{4,20},{5,21},{6,22},{7,23},{8,24},{9,... | collective-permute-start | bytes 737288 | tf_op jit(solution)/shard_map/ppermute | solution.py:323
  73.7 13.7 %collective-permute-start.1 = (f32[4,3,40,128]{3,2,1,0:T(8,128)S(1)}, f32[4,3,40,128]{3,2,1,0:T(8,128)S(1)}, u32[]{:S(2)}, u32[]{:S(2)}) collective-permute-start(f32[4,3,40,128]{3,2,1,0:T(8,128)S(1)} %get-tuple-element.15), channel_id=1, source_target_pairs={{0,8},{1,9},{2,10},{3,11},{4,12},{5,13},{6,14},{7,15},{8,16},{9,17... | collective-permute-start | bytes 737288 | tf_op jit(solution)/shard_map/ppermute | solution.py:323
  87.5 10.2 %collective-permute-start.6 = (f32[3,40,128]{2,1,0:T(8,128)S(1)}, f32[3,40,128]{2,1,0:T(8,128)S(1)}, u32[]{:S(2)}, u32[]{:S(2)}) collective-permute-start(f32[3,40,128]{2,1,0:T(8,128)S(1)} %get-tuple-element.19), channel_id=1, source_target_pairs={{0,6},{1,7},{2,0},{3,1},{4,2},{5,3},{6,4},{7,5},{8,14},{9,15},{10,... | collective-permute-start | bytes 184328 | tf_op jit(solution)/shard_map/ppermute | solution.py:323
  93.0 9.3 %collective-permute-start.5 = (f32[3,40,128]{2,1,0:T(8,128)S(1)}, f32[3,40,128]{2,1,0:T(8,128)S(1)}, u32[]{:S(2)}, u32[]{:S(2)}) collective-permute-start(f32[3,40,128]{2,1,0:T(8,128)S(1)} %get-tuple-element.20), channel_id=1, source_target_pairs={{0,4},{1,5},{2,6},{3,7},{4,0},{5,1},{6,2},{7,3},{8,12},{9,13},{10,... | collective-permute-start | bytes 184328 | tf_op jit(solution)/shard_map/ppermute | solution.py:323
  94.4 7.9 %collective-permute-start.4 = (f32[3,40,128]{2,1,0:T(8,128)S(1)}, f32[3,40,128]{2,1,0:T(8,128)S(1)}, u32[]{:S(2)}, u32[]{:S(2)}) collective-permute-start(f32[3,40,128]{2,1,0:T(8,128)S(1)} %get-tuple-element.18), channel_id=1, source_target_pairs={{0,2},{1,3},{2,4},{3,5},{4,6},{5,7},{6,0},{7,1},{8,10},{9,11},{10,... | collective-permute-start | bytes 184328 | tf_op jit(solution)/shard_map/ppermute | solution.py:323
  102.3 0.7 copy-start
